TPU v7x, 32 devices: a whole 2x2x4 slice. The times are simulated.
32 devices in a mesh: groups: 2 (over y), ens: 4 (over z), amp: 4 (over x, core).
Axes of the slice: x: 2, y: 2, z: 4, core: 2. Of those that a mesh axis runs over, the one named last changes fastest.
Arguments:
- states: bfloat16 [64, 2, 262144], P(('groups', 'ens'), None, 'amp'), parts along dimension 0, may hold values from -6 to 6
- layer_angles: int32 [64, 16, 7, 2], P(('groups', 'ens')), parts along dimension 0, may hold values from 0 to 63
- entangler: int32 [64, 16, 6], P(('groups', 'ens')), parts along dimension 0, may hold values 0 or 1
- global_angles: int32 [64, 2], P(('groups', 'ens')), parts along dimension 0, may hold values from 0 to 63
Outputs:
- correlations: float32 [2, 64, 32], P(None, ('groups', 'ens'), 'amp'), parts along dimension 1
There are 2 independent parts, one for each index of `groups`. A program takes and returns all parts, laid end to end along the dimension named above; each array names one. Nothing has to cross between parts.
All inputs are finite; a program needn't handle non-finite values. No bound on the sum of `entangler` on one device may be relied on, other than what follows from the above.
Results may differ from a plain program's by a relative error of at most 0.035.
Values may be sent and summed in bfloat16 or wider, within the bound.
A program may use at most 64 MiB of HBM per device.

v0:
```python
import math

import jax
import jax.numpy as jnp
from jax import lax
from jax.sharding import PartitionSpec as P

JOINED = 7
TABLE = 64


def from_partner(array, axis, bit):
    return lax.ppermute(array, axis, [(i, i ^ 1 << bit) for i in range(lax.axis_size(axis))])


def rotation(polar_index, azimuth_index):
    polar = polar_index.astype(jnp.float32) * (math.pi / TABLE)
    azimuth = azimuth_index.astype(jnp.float32) * (math.pi / TABLE)
    cos_polar = jnp.cos(polar)
    sin_polar = jnp.sin(polar)
    cos_azim = jnp.cos(azimuth)
    sin_azim = jnp.sin(azimuth)
    return (
        (cos_azim * cos_polar, -sin_azim * cos_polar),
        (-cos_azim * sin_polar, sin_azim * sin_polar),
        (cos_azim * sin_polar, sin_azim * sin_polar),
        (cos_azim * cos_polar, sin_azim * cos_polar),
    )


def pick_entry(gate, which, out_bit, in_bit):
    first = gate[0][which][:, None, None]
    second = gate[1][which][:, None, None]
    third = gate[2][which][:, None, None]
    fourth = gate[3][which][:, None, None]
    return jnp.where(
        out_bit == 0, jnp.where(in_bit == 0, first, second), jnp.where(in_bit == 0, third, fourth)
    )


def layer_weights(angles, links):
    order = 2**JOINED
    circuits = angles.shape[0]
    index_row = jnp.arange(order, dtype=jnp.int32)
    real_part = jnp.ones((circuits, order, order), jnp.float32)
    imag_part = jnp.zeros((circuits, order, order), jnp.float32)
    for qubit_index in range(JOINED):
        gate = rotation(angles[:, qubit_index, 0], angles[:, qubit_index, 1])
        bit_row = index_row // 2**qubit_index % 2
        out_bit = bit_row[None, :, None]
        in_bit = bit_row[None, None, :]
        factor_real = pick_entry(gate, 0, out_bit, in_bit)
        factor_imag = pick_entry(gate, 1, out_bit, in_bit)
        real_part, imag_part = (
            real_part * factor_real - imag_part * factor_imag,
            real_part * factor_imag + imag_part * factor_real,
        )
    sign_flip = jnp.ones((circuits, order), jnp.float32)
    for qubit_index in range(JOINED - 1):
        both_set = index_row // 2**qubit_index % 2 * (index_row // 2 ** (qubit_index + 1) % 2)
        flipped = links[:, qubit_index][:, None] * both_set[None, :]
        sign_flip = sign_flip * (1.0 - 2.0 * flipped.astype(jnp.float32))
    real_part = real_part * sign_flip[:, :, None]
    imag_part = imag_part * sign_flip[:, :, None]
    real_turned = jnp.transpose(real_part, (0, 2, 1))
    imag_turned = jnp.transpose(imag_part, (0, 2, 1))
    top_row = jnp.stack([real_turned, imag_turned], 1)
    bottom_row = jnp.stack([-imag_turned, real_turned], 1)
    return jnp.stack([top_row, bottom_row], 1).astype(jnp.bfloat16)


def bridge_signs(local):
    index_all = jnp.arange(local, dtype=jnp.int32)
    both_set = index_all // 2 ** (JOINED - 1) % 2 * (index_all // 2**JOINED % 2)
    return 1.0 - 2.0 * both_set.astype(jnp.float32)


def apply_layer(current, weights, upper_block):
    circuits, _, local = current.shape
    order = weights.shape[-1]
    if upper_block:
        reshaped = current.reshape(circuits, 2, local // (order * order), order, order)
        result = jnp.einsum(
            "cphnl,cpqnm->cqhml", reshaped, weights, preferred_element_type=jnp.float32
        )
    else:
        reshaped = current.reshape(circuits, 2, local // order, order)
        result = jnp.einsum(
            "cprn,cpqnm->cqrm", reshaped, weights, preferred_element_type=jnp.float32
        )
    result = result.reshape(circuits, 2, local) * bridge_signs(local)[None, None, :]
    return result.astype(jnp.bfloat16)


def scaled(coefficient, amplitudes):
    real_c = coefficient[0][:, None]
    imag_c = coefficient[1][:, None]
    return jnp.stack(
        [
            real_c * amplitudes[:, 0] - imag_c * amplitudes[:, 1],
            real_c * amplitudes[:, 1] + imag_c * amplitudes[:, 0],
        ],
        1,
    )


def choose_pair(upper_side, when_lower, when_upper):
    return (
        jnp.where(upper_side == 0, when_lower[0], when_upper[0]),
        jnp.where(upper_side == 0, when_lower[1], when_upper[1]),
    )


def pair_tile(mine, remote):
    products = jnp.einsum("ipa,jqa->pqij", mine, remote, preferred_element_type=jnp.float32)
    return jnp.stack([products[0, 0] + products[1, 1], products[0, 1] - products[1, 0]])


def body(states, layer_angles, entangler, global_angles):
    circuits = states.shape[0]

    def two_layers(pair_index, current):
        for offset, upper_block in ((0, False), (1, True)):
            layer = 2 * pair_index + offset
            angles = lax.dynamic_index_in_dim(layer_angles, layer, 1, keepdims=False)
            links = lax.dynamic_index_in_dim(entangler, layer, 1, keepdims=False)
            current = apply_layer(current, layer_weights(angles, links), upper_block)
        return current

    current = lax.fori_loop(0, layer_angles.shape[1] // 2, two_layers, states)
    swap_bit = lax.axis_size("amp").bit_length() - 2
    upper_side = lax.axis_index("amp") // 2**swap_bit % 2
    gate = rotation(global_angles[:, 0], global_angles[:, 1])
    partner = from_partner(current, "amp", swap_bit)
    coeff_self = choose_pair(upper_side, gate[0], gate[3])
    coeff_other = choose_pair(upper_side, gate[1], gate[2])
    final_states = (
        scaled(coeff_self, current.astype(jnp.float32))
        + scaled(coeff_other, partner.astype(jnp.float32))
    ).astype(jnp.bfloat16)
    own_block = lax.axis_index("ens")
    partials = pair_tile(final_states, lax.all_gather(final_states, "ens", axis=0, tiled=True))
    summed = lax.psum_scatter(partials, "amp", scatter_dimension=2, tiled=True)
    columns = summed.shape[2]
    row_index = own_block * circuits + jnp.arange(circuits, dtype=jnp.int32)
    column_index = lax.axis_index("amp") * columns + jnp.arange(columns, dtype=jnp.int32)
    off_diagonal = jnp.where(row_index[:, None] == column_index[None, :], 0.0, 1.0).astype(
        jnp.float32
    )
    amplitudes = states.shape[2] * lax.axis_size("amp")
    return summed * (off_diagonal / math.sqrt(amplitudes))[None]


def solution(mesh):
    return jax.shard_map(
        body,
        mesh=mesh,
        in_specs=(
            P(("groups", "ens"), None, "amp"),
            P(("groups", "ens"), None, None, None),
            P(("groups", "ens"), None, None),
            P(("groups", "ens"), None),
        ),
        out_specs=P(None, ("groups", "ens"), "amp"),
        check_vma=False,
    )
```

profile of v0, /device:TPU:0, one launch (start us, length us, event | category | flops | bytes accessed | tf_op | source)
XLA Modules:
  0.0 623.5 jit_solution(723011997608231308)
XLA Ops:
  11.2 380.7 %while.16 = (s32[]{:T(128)}, bf16[8,2,65536]{2,1,0:T(2,128)(2,1)}, s32[8,16,7,2]{0,3,2,1:T(2,128)S(1)}, s32[8,16,6]{2,0,1:T(8,128)S(1)}, s32[]{:T(128)}, /*index=5*/s32[]{:T(128)}, s32[]{:T(128)}, s32[]{:T(128)}, s32[]{:T(128)}) while((s32[]{:T(128)}, bf16[8,2,65536]{2,1,0:T(2,128)(2,1)}, s32[8,16,7,2]{0,3,2,1:T(2,128)S(1)}, ...), condition=%wide.region_1.2_spmd, body=%wide.region_0.1_spmd.sunk | while | flops 1127635200 | bytes 59695824 | solution.py:130
  25.8 5.2 reshape.4718
  31.1 5.3 copy.51
  46.0 7.6 %reshape.4719 = f32[8,2,65536]{2,1,0:T(2,128)} reshape(f32[8,2,4,128,128]{4,3,2,1,0:T(8,128)} %convolution_bitcast_fusion.5) | data formatting | bytes 8388608 | tf_op jit(solution)/shard_map/while/body/eval_jaxpr/reshape | solution.py:91
  73.4 5.2 reshape.4718
  78.6 5.3 copy.51
  93.6 7.6 %reshape.4719 = f32[8,2,65536]{2,1,0:T(2,128)} reshape(f32[8,2,4,128,128]{4,3,2,1,0:T(8,128)} %convolution_bitcast_fusion.5) | data formatting | bytes 8388608 | tf_op jit(solution)/shard_map/while/body/eval_jaxpr/reshape | solution.py:91
  126.2 5.3 copy.51
  141.2 7.6 %reshape.4719 = f32[8,2,65536]{2,1,0:T(2,128)} reshape(f32[8,2,4,128,128]{4,3,2,1,0:T(8,128)} %convolution_bitcast_fusion.5) | data formatting | bytes 8388608 | tf_op jit(solution)/shard_map/while/body/eval_jaxpr/reshape | solution.py:91
  173.8 5.3 copy.51
  188.7 7.6 %reshape.4719 = f32[8,2,65536]{2,1,0:T(2,128)} reshape(f32[8,2,4,128,128]{4,3,2,1,0:T(8,128)} %convolution_bitcast_fusion.5) | data formatting | bytes 8388608 | tf_op jit(solution)/shard_map/while/body/eval_jaxpr/reshape | solution.py:91
  221.4 5.3 copy.51
  236.3 7.6 %reshape.4719 = f32[8,2,65536]{2,1,0:T(2,128)} reshape(f32[8,2,4,128,128]{4,3,2,1,0:T(8,128)} %convolution_bitcast_fusion.5) | data formatting | bytes 8388608 | tf_op jit(solution)/shard_map/while/body/eval_jaxpr/reshape | solution.py:91
  269.0 5.3 copy.51
  283.9 7.6 %reshape.4719 = f32[8,2,65536]{2,1,0:T(2,128)} reshape(f32[8,2,4,128,128]{4,3,2,1,0:T(8,128)} %convolution_bitcast_fusion.5) | data formatting | bytes 8388608 | tf_op jit(solution)/shard_map/while/body/eval_jaxpr/reshape | solution.py:91
  316.6 5.3 copy.51
  331.5 7.6 %reshape.4719 = f32[8,2,65536]{2,1,0:T(2,128)} reshape(f32[8,2,4,128,128]{4,3,2,1,0:T(8,128)} %convolution_bitcast_fusion.5) | data formatting | bytes 8388608 | tf_op jit(solution)/shard_map/while/body/eval_jaxpr/reshape | solution.py:91
  364.2 5.3 copy.51
  379.1 7.6 %reshape.4719 = f32[8,2,65536]{2,1,0:T(2,128)} reshape(f32[8,2,4,128,128]{4,3,2,1,0:T(8,128)} %convolution_bitcast_fusion.5) | data formatting | bytes 8388608 | tf_op jit(solution)/shard_map/while/body/eval_jaxpr/reshape | solution.py:91
  391.9 5.5 fusion.174
  403.2 43.0 %collective-permute-done = bf16[8,2,65536]{2,0,1:T(8,128)(2,1)S(1)} collective-permute-done((bf16[8,2,65536]{2,0,1:T(8,128)(2,1)}, bf16[8,2,65536]{2,0,1:T(8,128)(2,1)S(1)}, u32[]{:S(2)}, u32[]{:S(2)}) %collective-permute-start) | collective-permute-done | bytes 2097184 | tf_op jit(solution)/shard_map/ppermute | solution.py:13
  450.8 149.3 %all-gather.2.cloned.1.call-done = bf16[32,2,65536]{2,0,1:T(8,128)(2,1)} async-done(((bf16[8,2,65536]{2,0,1:T(8,128)(2,1)}), bf16[32,2,65536]{2,0,1:T(8,128)(2,1)}) %all-gather.2.cloned.1.call-update) | async-done | bytes 8388624 | tf_op jit(solution)/shard_map/all_gather | solution.py:142
  600.1 8.9 %fusion.160 = f32[2,2,8,32]{3,2,0,1:T(8,128)S(1)} fusion(bf16[8,2,65536]{2,0,1:T(8,128)(2,1)S(1)} %copy-done, bf16[32,2,65536]{2,0,1:T(8,128)(2,1)} %all-gather.2.cloned.1.call-done), kind=kOutput, calls=%fused_computation.486 | convolution fusion | flops 134217728 | bytes 10489856 | tf_op jit(solution)/shard_map/ipa,jqa->pqij/dot_general | solution.py:115
  609.0 6.9 %all-reduce = f32[2,8,32]{2,1,0:T(8,128)S(1)} all-reduce(f32[2,8,32]{2,1,0:T(8,128)S(1)} %pad_maximum_fusion), channel_id=2, replica_groups=mesh['groups'=2,'ens'=4,'amp'=4] {'amp'}, use_global_device_ids=true, to_apply=%region_2.3.clone | all-reduce | flops 512 | bytes 4096
  (370 shorter events, 280.0 us)
Async XLA Ops:
  6.5 4.4 copy-start.1
  6.5 4.6 copy-start.2
  6.5 593.6 %all-gather.2.cloned.1.call-start = ((), (), s32[]{:S(2)}) async-start(), calls=%async_computation | async-start | bytes 10485760 | tf_op jit(solution)/shard_map/all_gather | solution.py:142
  391.9 8.5 %copy-start.3 = (s32[8,2]{0,1:T(2,128)S(1)}, s32[8,2]{0,1:T(2,128)}, u32[]{:S(2)}) copy-start(s32[8,2]{0,1:T(2,128)} %param.9) | copy-start | bytes 196
  397.5 48.8 %collective-permute-start = (bf16[8,2,65536]{2,0,1:T(8,128)(2,1)}, bf16[8,2,65536]{2,0,1:T(8,128)(2,1)S(1)}, u32[]{:S(2)}, u32[]{:S(2)}) collective-permute-start(bf16[8,2,65536]{2,0,1:T(8,128)(2,1)} %get-tuple-element.409), channel_id=1, source_target_pairs={{0,2},{1,3},{2,0},{3,1},{4,6},{5,7},{6,4},{7,5},{8,10},{9,11},{10,... | collective-permute-start | bytes 6291464 | tf_op jit(solution)/shard_map/ppermute | solution.py:13
  448.8 0.7 copy-start.4
  448.8 151.3 %copy-start = (bf16[8,2,65536]{2,0,1:T(8,128)(2,1)S(1)}, bf16[8,2,65536]{2,0,1:T(8,128)(2,1)}, u32[]{:S(2)}) copy-start(bf16[8,2,65536]{2,0,1:T(8,128)(2,1)} %fusion.158) | copy-start | bytes 6291460
Sparse Core Ops, SparseCore 0:
  448.9 151.1 all-gather.1
where the time goes:
time: 628 us; the launch traced here: 624 us
  local copies, waits for them, and re-layouts  193 us (31%)
  waiting for transfers between devices  192 us (31%)
  other arithmetic  141 us (22%)
  matrix products  70.5 us (11%)
  between operations  14.1 us (2%)
  blocking collectives  6.95 us (1%)
    all_gather x1, waiting for transfers between devices, body(): lax.all_gather(final_states, 'ens', axis=0, tiled=True)  149 us
    reshape x24, local copies, waits for them, and re-layouts, apply_layer(): result.reshape(circuits, 2, local) * bridge_signs(local)[None, None, :]  145 us
    another operation x48, other arithmetic  67 us
    ppermute x1, waiting for transfers between devices, from_partner(): lax.ppermute(array, axis, [(i, i ^ 1 << bit) for i in range(lax.axis_size...  43 us
    convert_element_type x8, other arithmetic, apply_layer(): return result.astype(jnp.bfloat16)  40.9 us
    dot_general x8, matrix products, apply_layer(): jnp.einsum('cphnl,cpqnm->cqhml', reshaped, weights, preferred_element_typ...  39.6 us
    reshape x8, local copies, waits for them, and re-layouts, apply_layer(): reshaped = current.reshape(circuits, 2, local // order, order)  39.2 us
    dot_general x8, matrix products, apply_layer(): jnp.einsum('cprn,cpqnm->cqrm', reshaped, weights, preferred_element_type=...  22 us
  transfers between devices with their start and end apart: 2, of which 2 were waited for; matrix products, arithmetic and copies ran while one was open for 1% of the time, Pallas kernels for 0%

commit v1 on v0

v1 whole, which is shorter than its diff:
```python
import functools
import math

import jax
import jax.numpy as jnp
from jax import lax
from jax.experimental import pallas as pl
from jax.experimental.pallas import tpu as pltpu
from jax.sharding import PartitionSpec as P

JOINED = 7
TABLE = 64
ORDER = 2**JOINED
LOW = 3
GROUP = 2


def from_partner(array, axis, bit):
    return lax.ppermute(array, axis, [(i, i ^ 1 << bit) for i in range(lax.axis_size(axis))])


def rotation(polar_index, azimuth_index):
    polar = polar_index.astype(jnp.float32) * (math.pi / TABLE)
    azimuth = azimuth_index.astype(jnp.float32) * (math.pi / TABLE)
    cos_polar = jnp.cos(polar)
    sin_polar = jnp.sin(polar)
    cos_azim = jnp.cos(azimuth)
    sin_azim = jnp.sin(azimuth)
    return (
        (cos_azim * cos_polar, -sin_azim * cos_polar),
        (-cos_azim * sin_polar, sin_azim * sin_polar),
        (cos_azim * sin_polar, sin_azim * sin_polar),
        (cos_azim * cos_polar, sin_azim * cos_polar),
    )


def bit_of(shape, dim, bit, shift=0):
    return (lax.broadcasted_iota(jnp.int32, shape, dim) >> (bit - shift)) & 1


def part_factor(cos_ref, sin_ref, flip_ref, at, upper, high):
    qubits = range(LOW, JOINED) if high else range(LOW)
    shape = (2 ** len(qubits), ORDER)
    shift = LOW if high else 0
    row = {k: bit_of(shape, 0, k, shift) for k in qubits}
    lane = {k: bit_of(shape, 1, k) for k in range(JOINED)}
    out = row if upper else lane
    real = imag = None
    turn = None
    for k in qubits:
        cos_t, sin_t = cos_ref[at * 14 + 2 * k], sin_ref[at * 14 + 2 * k]
        cos_f, sin_f = cos_ref[at * 14 + 2 * k + 1], sin_ref[at * 14 + 2 * k + 1]
        side = (2 * out[k] - 1).astype(jnp.float32)
        factor = jnp.where(row[k] == lane[k], cos_t, side * sin_t)
        turn = factor if turn is None else turn * factor
        step = side * sin_f
        if real is None:
            real, imag = jnp.full(shape, cos_f), step
        else:
            real, imag = real * cos_f - imag * step, real * step + imag * cos_f
    for k in range(JOINED - 1):
        inside = k in qubits and k + 1 in qubits
        if inside or (not upper and not high and k == LOW - 1):
            turn = jnp.where(out[k] * out[k + 1] == 1, flip_ref[at * 6 + k] * turn, turn)
    return real * turn, imag * turn


def build(cos_ref, sin_ref, flip_ref, at, upper, w_ref):
    low_real, low_imag = part_factor(cos_ref, sin_ref, flip_ref, at, upper, False)
    high_real, high_imag = part_factor(cos_ref, sin_ref, flip_ref, at, upper, True)
    lows = [(low_real, low_imag)] * 2
    if upper:
        crossed = bit_of(low_real.shape, 0, LOW - 1) == 1
        flip = flip_ref[at * 6 + LOW - 1]
        lows[1] = tuple(jnp.where(crossed, flip * v, v) for v in lows[0])
    for pair in range(ORDER // 16):
        reals, imags = [], []
        for odd in range(2):
            r = 2 * pair + odd
            a_real = jnp.broadcast_to(high_real[r : r + 1], (8, ORDER))
            a_imag = jnp.broadcast_to(high_imag[r : r + 1], (8, ORDER))
            b_real, b_imag = lows[odd]
            reals.append(a_real * b_real - a_imag * b_imag)
            imags.append(a_real * b_imag + a_imag * b_real)
        real = jnp.concatenate(reals, 0)
        imag = jnp.concatenate(imags, 0)
        plus, minus = imag.astype(jnp.bfloat16), (-imag).astype(jnp.bfloat16)
        real = real.astype(jnp.bfloat16)
        top, bottom = (minus, plus) if upper else (plus, minus)
        rows = pl.ds(16 * pair, 16)
        rows_below = pl.ds(ORDER + 16 * pair, 16)
        w_ref[rows, :ORDER] = real
        w_ref[rows, ORDER:] = top
        w_ref[rows_below, :ORDER] = bottom
        w_ref[rows_below, ORDER:] = real


def bridge(values):
    rows, columns = values.shape
    shape = (1, 8, columns)
    odd = bit_of(shape, 1, 0) * bit_of(shape, 2, JOINED - 1)
    sign = (1 - 2 * odd).astype(jnp.float32)
    return (values.reshape(rows // 8, 8, columns) * sign).reshape(rows, columns)


def run_layers(first, layers, cos_ref, sin_ref, flip_ref, x_refs, t_refs, wl_ref, wu_ref, s_ref):
    rows = t_refs[0].shape[0]
    blocks = rows // ORDER
    many = len(t_refs)
    for i in range(many):
        t_refs[i][:, :ORDER] = x_refs[i][0]
        t_refs[i][:, ORDER:] = x_refs[i][1]
        build(cos_ref, sin_ref, flip_ref, (first + i) * layers, False, wl_ref.at[i])

    def two(pair, carry):
        layer = 2 * pair
        following = jnp.minimum(layer + 2, layers - 2)
        for i in range(many):
            at = (first + i) * layers
            y = jnp.dot(t_refs[i][...], wl_ref[i], preferred_element_type=jnp.float32)
            y = bridge(y).astype(jnp.bfloat16)
            for b in range(blocks):
                for p in range(2):
                    s_ref[i, p * ORDER : (p + 1) * ORDER, b * ORDER : (b + 1) * ORDER] = y[
                        b * ORDER : (b + 1) * ORDER, p * ORDER : (p + 1) * ORDER
                    ]
            build(cos_ref, sin_ref, flip_ref, at + layer + 1, True, wu_ref.at[i])
        for i in range(many):
            at = (first + i) * layers
            y = jnp.dot(wu_ref[i], s_ref[i], preferred_element_type=jnp.float32)
            y = bridge(y).astype(jnp.bfloat16)
            for b in range(blocks):
                for p in range(2):
                    t_refs[i][b * ORDER : (b + 1) * ORDER, p * ORDER : (p + 1) * ORDER] = y[
                        p * ORDER : (p + 1) * ORDER, b * ORDER : (b + 1) * ORDER
                    ]
            build(cos_ref, sin_ref, flip_ref, at + following, False, wl_ref.at[i])
        return carry

    lax.fori_loop(0, layers // 2, two, 0)


def layers_scratch(rows):
    return [
        pltpu.VMEM((GROUP, 2 * ORDER, 2 * ORDER), jnp.bfloat16),
        pltpu.VMEM((GROUP, 2 * ORDER, 2 * ORDER), jnp.bfloat16),
        pltpu.VMEM((GROUP, 2 * ORDER, rows), jnp.bfloat16),
    ]


def layers_kernel(layers, cos_ref, sin_ref, flip_ref, x_ref, t_ref, wl_ref, wu_ref, s_ref):
    first = pl.program_id(0) * GROUP
    run_layers(
        first, layers, cos_ref, sin_ref, flip_ref,
        [x_ref.at[i] for i in range(GROUP)], [t_ref.at[i] for i in range(GROUP)],
        wl_ref, wu_ref, s_ref,
    )


def small_tables(layer_angles, entangler):
    angle = layer_angles.astype(jnp.float32).reshape(-1) * (math.pi / TABLE)
    flip = 1.0 - 2.0 * entangler.astype(jnp.float32).reshape(-1)
    return jnp.cos(angle), jnp.sin(angle), flip


def all_layers(states, layer_angles, entangler):
    circuits, _, local = states.shape
    rows = local // ORDER
    layers = layer_angles.shape[1]
    smem = pl.BlockSpec(memory_space=pltpu.SMEM)
    return pl.pallas_call(
        functools.partial(layers_kernel, layers),
        grid=(circuits // GROUP,),
        out_shape=jax.ShapeDtypeStruct((circuits, rows, 2 * ORDER), jnp.bfloat16),
        in_specs=[smem, smem, smem, pl.BlockSpec((GROUP, 2, rows, ORDER), lambda g: (g, 0, 0, 0))],
        out_specs=pl.BlockSpec((GROUP, rows, 2 * ORDER), lambda g: (g, 0, 0)),
        scratch_shapes=layers_scratch(rows),
        compiler_params=pltpu.CompilerParams(vmem_limit_bytes=32 << 20),
    )(*small_tables(layer_angles, entangler), states.reshape(circuits, 2, rows, ORDER))


def scaled(coefficient, amplitudes):
    real_c = coefficient[0][:, None]
    imag_c = coefficient[1][:, None]
    return jnp.stack(
        [
            real_c * amplitudes[:, 0] - imag_c * amplitudes[:, 1],
            real_c * amplitudes[:, 1] + imag_c * amplitudes[:, 0],
        ],
        1,
    )


def choose_pair(upper_side, when_lower, when_upper):
    return (
        jnp.where(upper_side == 0, when_lower[0], when_upper[0]),
        jnp.where(upper_side == 0, when_lower[1], when_upper[1]),
    )


def pair_tile(mine, remote):
    products = jnp.einsum("ipa,jqa->pqij", mine, remote, preferred_element_type=jnp.float32)
    return jnp.stack([products[0, 0] + products[1, 1], products[0, 1] - products[1, 0]])


def body(states, layer_angles, entangler, global_angles):
    circuits = states.shape[0]

    turned = all_layers(states, layer_angles, entangler).reshape(circuits, -1, 2, ORDER)
    current = jnp.swapaxes(turned, 1, 2).reshape(states.shape)
    swap_bit = lax.axis_size("amp").bit_length() - 2
    upper_side = lax.axis_index("amp") // 2**swap_bit % 2
    gate = rotation(global_angles[:, 0], global_angles[:, 1])
    partner = from_partner(current, "amp", swap_bit)
    coeff_self = choose_pair(upper_side, gate[0], gate[3])
    coeff_other = choose_pair(upper_side, gate[1], gate[2])
    final_states = (
        scaled(coeff_self, current.astype(jnp.float32))
        + scaled(coeff_other, partner.astype(jnp.float32))
    ).astype(jnp.bfloat16)
    own_block = lax.axis_index("ens")
    partials = pair_tile(final_states, lax.all_gather(final_states, "ens", axis=0, tiled=True))
    summed = lax.psum_scatter(partials, "amp", scatter_dimension=2, tiled=True)
    columns = summed.shape[2]
    row_index = own_block * circuits + jnp.arange(circuits, dtype=jnp.int32)
    column_index = lax.axis_index("amp") * columns + jnp.arange(columns, dtype=jnp.int32)
    off_diagonal = jnp.where(row_index[:, None] == column_index[None, :], 0.0, 1.0).astype(
        jnp.float32
    )
    amplitudes = states.shape[2] * lax.axis_size("amp")
    return summed * (off_diagonal / math.sqrt(amplitudes))[None]


def solution(mesh):
    return jax.shard_map(
        body,
        mesh=mesh,
        in_specs=(
            P(("groups", "ens"), None, "amp"),
            P(("groups", "ens"), None, None, None),
            P(("groups", "ens"), None, None),
            P(("groups", "ens"), None),
        ),
        out_specs=P(None, ("groups", "ens"), "amp"),
        check_vma=False,
    )
```

time: 628 us -> 270 us (0.43)
  local copies, waits for them, and re-layouts: 193 us -> 10.2 us
  other arithmetic: 141 us -> 13.4 us
  matrix products: 70.5 us -> 8.87 us
  Pallas kernels: 0 us -> 21.2 us
    reshape x32 -> x2, local copies, waits for them, and re-layouts: 184 us -> 5.94 us  [the longest x1 3.87 us: all_layers(): states.reshape(circuits, 2, rows, ORDER)]
    another operation x64 -> x0, other arithmetic: 68.2 us -> none
    dot_general x16 -> x0, matrix products: 61.6 us -> none  [the longest x8 39.6 us: apply_layer(): jnp.einsum('cphnl,cpqnm->cqhml', reshaped, weights, preferred_element_typ...]
    convert_element_type x8 -> x0, other arithmetic: 40.9 us -> none  [apply_layer(): return result.astype(jnp.bfloat16)]
    pallas_call x0 -> x1, Pallas kernels: none -> 21.2 us  [all_layers(): pl.pallas_call(functools.partial(layers_kernel, layers), grid=(circuits /...]
    broadcast_in_dim x80 -> x0, other arithmetic: 10.8 us -> none  [the longest x64 8.33 us: pick_entry(): jnp.where(in_bit == 0, first, second)]
where the time goes in v1:
time: 270 us
  waiting for transfers between devices  192 us (71%)
  Pallas kernels  21.2 us (8%)
  between operations  14.1 us (5%)
  other arithmetic  13.4 us (5%)
  local copies, waits for them, and re-layouts  10.2 us (4%)
  matrix products  8.87 us (3%)
  blocking collectives  6.95 us (3%)
  starting transfers between devices  2.94 us (1%)
    all_gather x1, waiting for transfers between devices, body(): lax.all_gather(final_states, 'ens', axis=0, tiled=True)  149 us
    ppermute x1, waiting for transfers between devices, from_partner(): lax.ppermute(array, axis, [(i, i ^ 1 << bit) for i in range(lax.axis_size...  43 us
    pallas_call x1, Pallas kernels, all_layers(): pl.pallas_call(functools.partial(layers_kernel, layers), grid=(circuits /...  21.2 us
    dot_general x1, matrix products, pair_tile(): jnp.einsum('ipa,jqa->pqij', mine, remote, preferred_element_type=jnp.floa...  8.87 us
    unnamed x1, blocking collectives  6.95 us
    reshape x1, other arithmetic, body(): current = jnp.swapaxes(turned, 1, 2).reshape(states.shape)  5.49 us
  transfers between devices with their start and end apart: 2, of which 2 were waited for; matrix products, arithmetic and copies ran while one was open for 1% of the time, Pallas kernels for 0%

profile of v1, /device:TPU:0, one launch (start us, length us, event | category | flops | bytes accessed | tf_op | source)
XLA Modules:
  0.0 270.1 jit_solution(17562134216897866661)
XLA Ops:
  6.5 1.8 fusion.9
  8.3 0.4 copy.14
  8.7 0.2 cos.18.cos_ref
  8.9 0.4 copy.15
  9.4 0.2 sin.16.sin_ref
  9.6 0.1 copy.16
  9.7 0.1 sub.35.flip_ref
  9.9 3.9 %reshape.140.x_ref = bf16[8,2,512,128]{3,2,1,0:T(8,128)(2,1)} reshape(bf16[8,2,65536]{2,1,0:T(2,128)(2,1)S(1)} %copy-done.2) | data formatting | bytes 4194304 | tf_op jit(solution)/shard_map/reshape | solution.py:179
  13.7 1.6 copy-done
  15.3 21.2 %shard_map.46 = bf16[8,512,256]{2,1,0:T(8,128)(2,1)S(1)} custom-call(f32[1792]{0:T(1024)S(1)} %cos.18.cos_ref, f32[1792]{0:T(1024)S(1)} %sin.16.sin_ref, f32[768]{0:T(1024)S(1)} %sub.35.flip_ref, bf16[8,2,512,128]{3,2,1,0:T(8,128)(2,1)S(1)} %copy-done), custom_call_target="tpu_custom_call" | custom-call | tf_op jit(solution)/shard_map/pallas_call | solution.py:171
  36.5 2.1 reshape.141
  38.6 5.5 %copy_bitcast_fusion = (bf16[8,2,65536]{2,0,1:T(8,128)(2,1)}, f32[8,2,65536]{2,0,1:T(8,128)}) fusion(bf16[8,2,512,128]{3,1,2,0:T(2,128)(2,1)} %bitcast.44), kind=kLoop, calls=%fused_computation.5 | loop fusion | flops 1048576 | bytes 8388608 | tf_op jit(solution)/shard_map/reshape | solution.py:210
  44.1 2.9 %collective-permute-start = (bf16[8,2,65536]{2,0,1:T(8,128)(2,1)}, bf16[8,2,65536]{2,0,1:T(8,128)(2,1)S(1)}, u32[]{:S(2)}, u32[]{:S(2)}) collective-permute-start(bf16[8,2,65536]{2,0,1:T(8,128)(2,1)} %get-tuple-element.9), channel_id=1, source_target_pairs={{0,2},{1,3},{2,0},{3,1},{4,6},{5,7},{6,4},{7,5},{8,10},{9,11},{10,... | collective-permute-start | bytes 6291464 | tf_op jit(solution)/shard_map/ppermute | solution.py:19
  47.1 2.7 %multiply_subtract_fusion.1 = (f32[8,1,65536]{2,0,1:T(8,128)S(1)}, f32[8,1,65536]{2,0,1:T(8,128)S(1)}) fusion(f32[8,2,65536]{2,0,1:T(8,128)} %get-tuple-element.10, f32[8]{0:T(128)S(1)} %get-tuple-element.16, f32[8]{0:T(128)S(1)} %get-tuple-element.15), kind=kLoop, calls=%fused_computation.9 | loop fusion | flops 3145728 | bytes 8388672 | tf_op jit(solution)/shard_map/sub | solution.py:187
  49.8 43.0 %collective-permute-done = bf16[8,2,65536]{2,0,1:T(8,128)(2,1)S(1)} collective-permute-done((bf16[8,2,65536]{2,0,1:T(8,128)(2,1)}, bf16[8,2,65536]{2,0,1:T(8,128)(2,1)S(1)}, u32[]{:S(2)}, u32[]{:S(2)}) %collective-permute-start) | collective-permute-done | bytes 2097184 | tf_op jit(solution)/shard_map/ppermute | solution.py:19
  92.9 0.3 convert_element_type.34
  93.2 0.5 multiply_subtract_fusion
  93.7 1.7 fusion.2
  95.5 0.6 copy-done.5
  96.1 0.6 dynamic-slice
  97.4 149.3 %all-gather.2.cloned.1.call-done = bf16[32,2,65536]{2,0,1:T(8,128)(2,1)} async-done(((bf16[8,2,65536]{2,0,1:T(8,128)(2,1)}), bf16[32,2,65536]{2,0,1:T(8,128)(2,1)}) %all-gather.2.cloned.1.call-update) | async-done | bytes 8388624 | tf_op jit(solution)/shard_map/all_gather | solution.py:222
  246.7 8.9 %fusion.4 = f32[2,2,8,32]{3,2,0,1:T(8,128)S(1)} fusion(bf16[8,2,65536]{2,0,1:T(8,128)(2,1)S(1)} %copy-done.1, bf16[32,2,65536]{2,0,1:T(8,128)(2,1)} %all-gather.2.cloned.1.call-done), kind=kOutput, calls=%fused_computation.10 | convolution fusion | flops 134217728 | bytes 10489856 | tf_op jit(solution)/shard_map/ipa,jqa->pqij/dot_general | solution.py:202
  255.6 6.9 %all-reduce = f32[2,8,32]{2,1,0:T(8,128)S(1)} all-reduce(f32[2,8,32]{2,1,0:T(8,128)S(1)} %pad_maximum_fusion), channel_id=2, replica_groups=mesh['groups'=2,'ens'=4,'amp'=4] {'amp'}, use_global_device_ids=true, to_apply=%region_0.1.clone | all-reduce | flops 512 | bytes 4096
  262.6 0.7 dynamic-slice_multiply_fusion
  (19 shorter events, 0.2 us)
Async XLA Ops:
  6.5 3.0 %copy-start.3 = (s32[8,16,6]{1,0,2:T(8,128)S(1)}, s32[8,16,6]{1,0,2:T(8,128)}, u32[]{:S(2)}) copy-start(s32[8,16,6]{1,0,2:T(8,128)} %param.6) | copy-start | bytes 9220
  6.5 3.3 %copy-start.2 = (bf16[8,2,65536]{2,1,0:T(2,128)(2,1)S(1)}, bf16[8,2,65536]{2,1,0:T(2,128)(2,1)}, u32[]{:S(2)}) copy-start(bf16[8,2,65536]{2,1,0:T(2,128)(2,1)} %param.4) | copy-start | bytes 6291460
  6.5 240.2 %all-gather.2.cloned.1.call-start = ((), (), s32[]{:S(2)}) async-start(), calls=%async_computation | async-start | bytes 10485760 | tf_op jit(solution)/shard_map/all_gather | solution.py:222
  13.7 1.6 copy-start
  38.6 8.4 %copy-start.4 = (s32[8,2]{0,1:T(2,128)S(1)}, s32[8,2]{0,1:T(2,128)}, u32[]{:S(2)}) copy-start(s32[8,2]{0,1:T(2,128)} %param.7) | copy-start | bytes 196
  44.1 48.8 %collective-permute-start = (bf16[8,2,65536]{2,0,1:T(8,128)(2,1)}, bf16[8,2,65536]{2,0,1:T(8,128)(2,1)S(1)}, u32[]{:S(2)}, u32[]{:S(2)}) collective-permute-start(bf16[8,2,65536]{2,0,1:T(8,128)(2,1)} %get-tuple-element.9), channel_id=1, source_target_pairs={{0,2},{1,3},{2,0},{3,1},{4,6},{5,7},{6,4},{7,5},{8,10},{9,11},{10,... | collective-permute-start | bytes 6291464 | tf_op jit(solution)/shard_map/ppermute | solution.py:19
  95.4 0.7 copy-start.5
  95.4 151.3 %copy-start.1 = (bf16[8,2,65536]{2,0,1:T(8,128)(2,1)S(1)}, bf16[8,2,65536]{2,0,1:T(8,128)(2,1)}, u32[]{:S(2)}) copy-start(bf16[8,2,65536]{2,0,1:T(8,128)(2,1)} %fusion.2) | copy-start | bytes 6291460
Sparse Core Ops, SparseCore 0:
  95.6 151.1 all-gather.1

commit v2 on v1

--- a/solution.py
+++ b/solution.py
@@ -179,6 +179,235 @@
     )(*small_tables(layer_angles, entangler), states.reshape(circuits, 2, rows, ORDER))
 
 
+MESH_ID = pl.DeviceIdType.MESH
+
+
+def gate_pair(gate, low, high):
+    outs = []
+    for r in range(2):
+        a_real, a_imag, b_real, b_imag = (gate[4 * r + k : 4 * r + k + 1] for k in range(4))
+        real = a_real * low[0] - a_imag * low[1] + (b_real * high[0] - b_imag * high[1])
+        imag = a_real * low[1] + a_imag * low[0] + (b_real * high[1] + b_imag * high[0])
+        outs.append((real, imag))
+    return outs
+
+
+def fused_kernel(
+    layers, ens, amp,
+    cos_ref, sin_ref, flip_ref, gate_ref, x_ref, o_ref,
+    wl_ref, wu_ref, s_ref, t_ref, r_ref, c_ref, f_ref, h_ref, p_ref, q_ref,
+    send_sem, recv_sem, gate_send, gate_recv, sum_send, sum_recv,
+):
+    circuits, rows, _ = t_ref.shape
+    groups = circuits // GROUP
+    share = rows // (2 * ens)
+    parts = share // 16
+    bit = amp.bit_length() - 2
+    me = lax.axis_index("ens")
+    here = lax.axis_index("amp")
+    side = (here // 2**bit) % 2
+    rest = here - side * 2**bit
+
+    barrier = pltpu.get_barrier_semaphore()
+    everyone = [(k // amp, k % amp) for k in range(1, ens * amp)]
+    for e, a in everyone:
+        pl.semaphore_signal(
+            barrier, inc=1, device_id={"ens": (me + e) % ens, "amp": (here + a) % amp}, device_id_type=MESH_ID
+        )
+    pl.semaphore_wait(barrier, len(everyone))
+
+    def gate_copy(k, source):
+        return pltpu.make_async_remote_copy(
+            src_ref=gate_ref,
+            dst_ref=c_ref.at[pl.ds(source * circuits, circuits)],
+            send_sem=gate_send.at[k - 1],
+            recv_sem=gate_recv.at[k - 1],
+            device_id={"ens": (me + k) % ens},
+            device_id_type=MESH_ID,
+        )
+
+    for k in range(1, ens):
+        gate_copy(k, me).start()
+    c_ref[pl.ds(me * circuits, circuits)] = gate_ref[...]
+
+    peers = [(k // ens, k % ens) for k in range(1, 2 * ens)]
+
+    def piece(k, group, from_side, from_ens):
+        across, along = peers[k]
+        to_side = side + across - 2 * side * across
+        to_ens = (me + along) % ens
+        start = pl.multiple_of((to_side * ens + to_ens) * share, share)
+        return pltpu.make_async_remote_copy(
+            src_ref=t_ref.at[pl.ds(group * GROUP, GROUP), pl.ds(start, share)],
+            dst_ref=r_ref.at[from_side, pl.ds(from_ens * circuits + group * GROUP, GROUP)],
+            send_sem=send_sem.at[group, k],
+            recv_sem=recv_sem.at[group, k],
+            device_id={"ens": to_ens, "amp": to_side * 2**bit + rest},
+            device_id_type=MESH_ID,
+        )
+
+    def compute(group, carry):
+        first = group * GROUP
+        run_layers(
+            first, layers, cos_ref, sin_ref, flip_ref,
+            [x_ref.at[first + i] for i in range(GROUP)], [t_ref.at[first + i] for i in range(GROUP)],
+            wl_ref, wu_ref, s_ref,
+        )
+        for k in range(len(peers)):
+            piece(k, group, side, me).start()
+        own = pl.multiple_of((side * ens + me) * share, share)
+        for i in range(GROUP):
+            r_ref[side, me * circuits + first + i] = t_ref[first + i, pl.ds(own, share), :]
+        return carry
+
+    lax.fori_loop(0, groups, compute, 0)
+    for k in range(1, ens):
+        gate_copy(k, (me + ens - k) % ens).wait_recv()
+
+    def arrive(group, carry):
+        for k, (across, along) in enumerate(peers):
+            piece(k, group, side + across - 2 * side * across, (me + ens - along) % ens).wait_recv()
+
+        def one(step, inner):
+            which = (step // GROUP) * circuits + group * GROUP + step % GROUP
+            gate = c_ref[which]
+            low = r_ref[0, which].astype(jnp.float32)
+            high = r_ref[1, which].astype(jnp.float32)
+            outs = gate_pair(gate, (low[:, :ORDER], low[:, ORDER:]), (high[:, :ORDER], high[:, ORDER:]))
+            for x, (real, imag) in enumerate(outs):
+                real = real.astype(jnp.bfloat16)
+                minus = (-real).astype(jnp.bfloat16)
+                imag = imag.astype(jnp.bfloat16)
+                for part in range(parts):
+                    at = (x * parts + part) * 2 * ORDER
+                    take = slice(16 * part, 16 * part + 16)
+                    f_ref[which, :, at : at + ORDER] = real[take]
+                    f_ref[which, :, at + ORDER : at + 2 * ORDER] = imag[take]
+                    h_ref[which, :, at : at + ORDER] = imag[take]
+                    h_ref[which, :, at + ORDER : at + 2 * ORDER] = minus[take]
+            return inner
+
+        lax.fori_loop(0, ens * GROUP, one, 0)
+        return carry
+
+    lax.fori_loop(0, groups, arrive, 0)
+
+    total = ens * circuits
+    depth = f_ref.shape[2]
+    block = 16
+    p_ref[...] = jnp.zeros_like(p_ref)
+
+    def columns(step, carry):
+        rhs_at = pl.ds(step * block, block)
+        lhs = f_ref[...].reshape(total * 16, depth)
+        shape = (1, 16, block * 16)
+        same = lax.broadcasted_iota(jnp.int32, shape, 1) == lax.broadcasted_iota(jnp.int32, shape, 2) % 16
+        pick_shape = (block * 16, 128)
+        pick = lax.broadcasted_iota(jnp.int32, pick_shape, 0) // 16 + step * block
+        pick = (pick == lax.broadcasted_iota(jnp.int32, pick_shape, 1)).astype(jnp.float32)
+        for which, ref in enumerate((f_ref, h_ref)):
+            rhs = ref[rhs_at].reshape(block * 16, depth)
+            full = lax.dot_general(lhs, rhs, (((1,), (1,)), ((), ())), preferred_element_type=jnp.float32)
+            kept = jnp.where(same, full.reshape(total, 16, block * 16), 0.0).sum(1)
+            p_ref[which] += jnp.dot(
+                kept, pick, precision=lax.Precision.HIGHEST, preferred_element_type=jnp.float32
+            )
+        return carry
+
+    lax.fori_loop(0, total // block, columns, 0)
+
+    def slab(k):
+        e, a = everyone[k]
+        to = (me + e) % ens
+        return pltpu.make_async_remote_copy(
+            src_ref=p_ref.at[:, pl.ds(pl.multiple_of(to * circuits, circuits), circuits)],
+            dst_ref=q_ref.at[k],
+            send_sem=sum_send.at[k],
+            recv_sem=sum_recv.at[k],
+            device_id={"ens": to, "amp": (here + a) % amp},
+            device_id_type=MESH_ID,
+        )
+
+    for k in range(len(everyone)):
+        slab(k).start()
+    result = p_ref[:, pl.ds(pl.multiple_of(me * circuits, circuits), circuits), :]
+    for k in range(len(everyone)):
+        slab(k).wait_recv()
+        result = result + q_ref[k]
+    o_ref[...] = result
+    for k in range(len(everyone)):
+        slab(k).wait_send()
+    for k in range(1, ens):
+        gate_copy(k, me).wait_send()
+
+    def drain(group, carry):
+        for k in range(len(peers)):
+            piece(k, group, side, me).wait_send()
+        return carry
+
+    lax.fori_loop(0, groups, drain, 0)
+
+
+def fused(states, layer_angles, entangler, global_angles):
+    circuits, _, local = states.shape
+    rows = local // ORDER
+    layers = layer_angles.shape[1]
+    ens, amp = lax.axis_size("ens"), lax.axis_size("amp")
+    total = ens * circuits
+    share = rows // (2 * ens)
+    depth = 2 * (share // 16) * 2 * ORDER
+    gate = rotation(global_angles[:, 0], global_angles[:, 1])
+    coefficients = jnp.stack([part for entry in gate for part in entry], 1)
+    coefficients = jnp.broadcast_to(coefficients[:, :, None], (circuits, 8, 128))
+    smem = pl.BlockSpec(memory_space=pltpu.SMEM)
+    vmem = pl.BlockSpec(memory_space=pltpu.VMEM)
+    groups = circuits // GROUP
+    return pl.pallas_call(
+        functools.partial(fused_kernel, layers, ens, amp),
+        out_shape=jax.ShapeDtypeStruct((2, circuits, 128), jnp.float32),
+        in_specs=[smem, smem, smem, vmem, vmem],
+        out_specs=vmem,
+        scratch_shapes=layers_scratch(rows)
+        + [
+            pltpu.VMEM((circuits, rows, 2 * ORDER), jnp.bfloat16),
+            pltpu.VMEM((2, total, share, 2 * ORDER), jnp.bfloat16),
+            pltpu.VMEM((total, 8, 128), jnp.float32),
+            pltpu.VMEM((total, 16, depth), jnp.bfloat16),
+            pltpu.VMEM((total, 16, depth), jnp.bfloat16),
+            pltpu.VMEM((2, total, 128), jnp.float32),
+            pltpu.VMEM((ens * amp - 1, 2, circuits, 128), jnp.float32),
+            pltpu.SemaphoreType.DMA((groups, 2 * ens - 1)),
+            pltpu.SemaphoreType.DMA((groups, 2 * ens - 1)),
+            pltpu.SemaphoreType.DMA((ens - 1,)),
+            pltpu.SemaphoreType.DMA((ens - 1,)),
+            pltpu.SemaphoreType.DMA((ens * amp - 1,)),
+            pltpu.SemaphoreType.DMA((ens * amp - 1,)),
+        ],
+        compiler_params=pltpu.CompilerParams(
+            vmem_limit_bytes=48 << 20, collective_id=0, has_side_effects=True
+        ),
+    )(*small_tables(layer_angles, entangler), coefficients, states.reshape(circuits, 2, rows, ORDER))
+
+
+def finish(summed, states, circuits):
+    columns = lax.axis_size("ens") * circuits // lax.axis_size("amp")
+    row_index = lax.axis_index("ens") * circuits + jnp.arange(circuits, dtype=jnp.int32)
+    column_index = lax.axis_index("amp") * columns + jnp.arange(columns, dtype=jnp.int32)
+    off_diagonal = jnp.where(row_index[:, None] == column_index[None, :], 0.0, 1.0).astype(jnp.float32)
+    amplitudes = states.shape[2] * lax.axis_size("amp")
+    return summed * (off_diagonal / math.sqrt(amplitudes))[None]
+
+
+def fits(states):
+    circuits, _, local = states.shape
+    ens = lax.axis_size("ens")
+    rows = local // ORDER
+    return (
+        rows % (2 * ens * 16) == 0 and circuits % 8 == 0 and ens * circuits % 16 == 0
+        and ens * circuits <= 128 and lax.axis_size("amp") >= 2 and local <= 1 << 16 and ens > 1
+    )
+
+
 def scaled(coefficient, amplitudes):
     real_c = coefficient[0][:, None]
     imag_c = coefficient[1][:, None]
@@ -205,7 +434,11 @@
 
 def body(states, layer_angles, entangler, global_angles):
     circuits = states.shape[0]
-
+    if fits(states):
+        summed = fused(states, layer_angles, entangler, global_angles)
+        columns = lax.axis_size("ens") * circuits // lax.axis_size("amp")
+        summed = lax.dynamic_slice_in_dim(summed, lax.axis_index("amp") * columns, columns, 2)
+        return finish(summed, states, circuits)
     turned = all_layers(states, layer_angles, entangler).reshape(circuits, -1, 2, ORDER)
     current = jnp.swapaxes(turned, 1, 2).reshape(states.shape)
     swap_bit = lax.axis_size("amp").bit_length() - 2
@@ -218,17 +451,9 @@
         scaled(coeff_self, current.astype(jnp.float32))
         + scaled(coeff_other, partner.astype(jnp.float32))
     ).astype(jnp.bfloat16)
-    own_block = lax.axis_index("ens")
     partials = pair_tile(final_states, lax.all_gather(final_states, "ens", axis=0, tiled=True))
     summed = lax.psum_scatter(partials, "amp", scatter_dimension=2, tiled=True)
-    columns = summed.shape[2]
-    row_index = own_block * circuits + jnp.arange(circuits, dtype=jnp.int32)
-    column_index = lax.axis_index("amp") * columns + jnp.arange(columns, dtype=jnp.int32)
-    off_diagonal = jnp.where(row_index[:, None] == column_index[None, :], 0.0, 1.0).astype(
-        jnp.float32
-    )
-    amplitudes = states.shape[2] * lax.axis_size("amp")
-    return summed * (off_diagonal / math.sqrt(amplitudes))[None]
+    return finish(summed, states, circuits)
 
 
 def solution(mesh):

time: 270 us -> 80.4 us (0.30)
  waiting for transfers between devices: 192 us -> 0 us
  Pallas kernels: 21.2 us -> 71 us
  between operations: 14.1 us -> 0.08 us
  other arithmetic: 13.4 us -> 2.45 us
  matrix products: 8.87 us -> 0 us
  blocking collectives: 6.95 us -> 0 us
  local copies, waits for them, and re-layouts: 10.2 us -> 6.57 us
  starting transfers between devices: 2.94 us -> 0 us
    all_gather x1 -> x0, waiting for transfers between devices: 149 us -> none  [body(): lax.all_gather(final_states, 'ens', axis=0, tiled=True)]
    pallas_call x1, Pallas kernels: 21.2 us -> 71 us  [fused(): pl.pallas_call(functools.partial(fused_kernel, layers, ens, amp), out_sha...]
    ppermute x1 -> x0, waiting for transfers between devices: 43 us -> none  [from_partner(): lax.ppermute(array, axis, [(i, i ^ 1 << bit) for i in range(lax.axis_size...]
    dot_general x1 -> x0, matrix products: 8.87 us -> none  [pair_tile(): jnp.einsum('ipa,jqa->pqij', mine, remote, preferred_element_type=jnp.floa...]
    unnamed x1 -> x0, blocking collectives: 6.95 us -> none
    reshape x1 -> x0, other arithmetic: 5.49 us -> none  [body(): current = jnp.swapaxes(turned, 1, 2).reshape(states.shape)]
    sub x3 -> x0, other arithmetic: 3.24 us -> none  [the longest x2 3.23 us: scaled(): real_c * amplitudes[:, 0] - imag_c * amplitudes[:, 1]]
    ppermute x1 -> x0, starting transfers between devices: 2.94 us -> none  [from_partner(): lax.ppermute(array, axis, [(i, i ^ 1 << bit) for i in range(lax.axis_size...]
  transfers between devices with their start and end apart: 2 -> 0, of which waited for: 2 -> 0; matrix products, arithmetic and copies ran while one was open for 1% -> 0% of each run, Pallas kernels for 0% -> 0%
where the time goes in v2:
time: 80.4 us; the launch traced here: 80.1 us
  Pallas kernels  71 us (88%)
  local copies, waits for them, and re-layouts  6.57 us (8%)
  other arithmetic  2.45 us (3%)
    pallas_call x1, Pallas kernels, fused(): pl.pallas_call(functools.partial(fused_kernel, layers, ens, amp), out_sha...  71 us
    reshape x1, local copies, waits for them, and re-layouts, fused(): states.reshape(circuits, 2, rows, ORDER)  4.9 us
    sin x1, other arithmetic, small_tables(): return (jnp.cos(angle), jnp.sin(angle), flip)  1.64 us

profile of v2, /device:TPU:0, one launch (start us, length us, event | category | flops | bytes accessed | tf_op | source)
XLA Modules:
  0.0 80.1 jit_solution(18275009335079551169)
XLA Ops:
  0.0 0.0 copy-start
  0.0 0.0 copy-start.1
  0.0 1.6 %fusion = (f32[8,16,7,2]{1,3,2,0:T(2,128)S(1)}, f32[8,16,7,2]{1,3,2,0:T(2,128)S(1)}) fusion(s32[8,16,7,2]{1,3,2,0:T(2,128)} %param.5), kind=kLoop, calls=%fused_computation.1 | loop fusion | flops 3584 | bytes 21504 | tf_op jit(solution)/shard_map/sin | solution.py:163
  1.6 0.4 copy.6
  2.1 0.2 cos.18.cos_ref
  2.3 0.4 copy.7
  2.7 0.2 sin.18.sin_ref
  2.9 0.0 copy-done
  2.9 0.1 copy.8
  3.0 0.1 sub.10.flip_ref
  3.2 0.0 copy-done.1
  3.2 0.1 fusion.6
  3.3 0.1 copy.9
  3.3 0.1 broadcast_in_dim.10.gate_ref
  3.4 4.9 %reshape.51.x_ref = bf16[8,2,512,128]{3,2,1,0:T(8,128)(2,1)S(1)} reshape(bf16[8,2,65536]{2,1,0:T(2,128)(2,1)} %param.4) | data formatting | bytes 4194304 | tf_op jit(solution)/shard_map/reshape | solution.py:389
  8.3 71.0 %shard_map.46 = f32[2,8,128]{2,1,0:T(8,128)S(1)} custom-call(f32[1792]{0:T(1024)S(1)} %cos.18.cos_ref, f32[1792]{0:T(1024)S(1)} %sin.18.sin_ref, f32[768]{0:T(1024)S(1)} %sub.10.flip_ref, f32[8,8,128]{2,1,0:T(8,128)S(1)} %broadcast_in_dim.10.gate_ref, bf16[8,2,512,128]{3,2,1,0:T(8,128)(2,1)S(1)} %reshape.51.x_ref), custom_call_target="tpu_custom_call" | custom-call | tf_op jit(solution)/shard_map/pallas_call | solution.py:365
  79.4 0.1 select_multiply_fusion
  79.4 0.7 dynamic-slice_multiply_fusion
  (3 shorter events, 0.0 us)
Async XLA Ops:
  0.0 2.9 %copy-start = (s32[8,16,6]{1,0,2:T(8,128)S(1)}, s32[8,16,6]{1,0,2:T(8,128)}, u32[]{:S(2)}) copy-start(s32[8,16,6]{1,0,2:T(8,128)} %param.6) | copy-start | bytes 9220
  0.0 3.2 %copy-start.1 = (s32[8,2]{0,1:T(2,128)S(1)}, s32[8,2]{0,1:T(2,128)}, u32[]{:S(2)}) copy-start(s32[8,2]{0,1:T(2,128)} %param.7) | copy-start | bytes 196

commit v3 on v2

--- a/solution.py
+++ b/solution.py
@@ -195,7 +195,7 @@
 def fused_kernel(
     layers, ens, amp,
     cos_ref, sin_ref, flip_ref, gate_ref, x_ref, o_ref,
-    wl_ref, wu_ref, s_ref, t_ref, r_ref, c_ref, f_ref, h_ref, p_ref, q_ref,
+    wl_ref, wu_ref, s_ref, t_ref, r_ref, c_ref, f_ref, h_ref, l_ref, p_ref, q_ref,
     send_sem, recv_sem, gate_send, gate_recv, sum_send, sum_recv,
 ):
     circuits, rows, _ = t_ref.shape
@@ -264,11 +264,16 @@
     for k in range(1, ens):
         gate_copy(k, (me + ens - k) % ens).wait_recv()
 
-    def arrive(group, carry):
+    total = ens * circuits
+    fresh = ens * GROUP
+    depth = f_ref.shape[2]
+    l_ref[...] = jnp.zeros_like(l_ref)
+
+    for group in range(groups):
         for k, (across, along) in enumerate(peers):
             piece(k, group, side + across - 2 * side * across, (me + ens - along) % ens).wait_recv()
 
-        def one(step, inner):
+        def one(step, inner, group=group):
             which = (step // GROUP) * circuits + group * GROUP + step % GROUP
             gate = c_ref[which]
             low = r_ref[0, which].astype(jnp.float32)
@@ -281,40 +286,45 @@
                 for part in range(parts):
                     at = (x * parts + part) * 2 * ORDER
                     take = slice(16 * part, 16 * part + 16)
-                    f_ref[which, :, at : at + ORDER] = real[take]
-                    f_ref[which, :, at + ORDER : at + 2 * ORDER] = imag[take]
-                    h_ref[which, :, at : at + ORDER] = imag[take]
-                    h_ref[which, :, at + ORDER : at + 2 * ORDER] = minus[take]
+                    for ref, row in ((f_ref, group * fresh + step), (h_ref, step)):
+                        ref[row, :, at : at + ORDER] = real[take]
+                        ref[row, :, at + ORDER : at + 2 * ORDER] = imag[take]
+                    h_ref[fresh + step, :, at : at + ORDER] = imag[take]
+                    h_ref[fresh + step, :, at + ORDER : at + 2 * ORDER] = minus[take]
             return inner
 
-        lax.fori_loop(0, ens * GROUP, one, 0)
-        return carry
-
-    lax.fori_loop(0, groups, arrive, 0)
-
-    total = ens * circuits
-    depth = f_ref.shape[2]
-    block = 16
-    p_ref[...] = jnp.zeros_like(p_ref)
-
-    def columns(step, carry):
-        rhs_at = pl.ds(step * block, block)
-        lhs = f_ref[...].reshape(total * 16, depth)
-        shape = (1, 16, block * 16)
+        lax.fori_loop(0, fresh, one, 0)
+        known = (group + 1) * fresh
+        lhs = f_ref[:known].reshape(known * 16, depth)
+        rhs = h_ref[...].reshape(2 * fresh * 16, depth)
+        full = lax.dot_general(lhs, rhs, (((1,), (1,)), ((), ())), preferred_element_type=jnp.float32)
+        shape = (1, 16, 2 * fresh * 16)
         same = lax.broadcasted_iota(jnp.int32, shape, 1) == lax.broadcasted_iota(jnp.int32, shape, 2) % 16
-        pick_shape = (block * 16, 128)
-        pick = lax.broadcasted_iota(jnp.int32, pick_shape, 0) // 16 + step * block
+        kept = jnp.where(same, full.reshape(known, 16, 2 * fresh * 16), 0.0).sum(1)
+        pick_shape = (fresh * 16, 128)
+        pick = lax.broadcasted_iota(jnp.int32, pick_shape, 0) // 16 + group * fresh
         pick = (pick == lax.broadcasted_iota(jnp.int32, pick_shape, 1)).astype(jnp.float32)
-        for which, ref in enumerate((f_ref, h_ref)):
-            rhs = ref[rhs_at].reshape(block * 16, depth)
-            full = lax.dot_general(lhs, rhs, (((1,), (1,)), ((), ())), preferred_element_type=jnp.float32)
-            kept = jnp.where(same, full.reshape(total, 16, block * 16), 0.0).sum(1)
-            p_ref[which] += jnp.dot(
-                kept, pick, precision=lax.Precision.HIGHEST, preferred_element_type=jnp.float32
+        for which in range(2):
+            l_ref[which, :known] += jnp.dot(
+                kept[:, which * fresh * 16 : (which + 1) * fresh * 16], pick,
+                precision=lax.Precision.HIGHEST, preferred_element_type=jnp.float32,
             )
-        return carry
-
-    lax.fori_loop(0, total // block, columns, 0)
+
+    square = (128, 128)
+    row = lax.broadcasted_iota(jnp.int32, square, 0)
+    column = lax.broadcasted_iota(jnp.int32, square, 1)
+    place = (row % circuits // GROUP) * fresh + row // circuits * GROUP + row % GROUP
+    order = jnp.where((place == column) & (row < total), 1.0, 0.0)
+    for which in range(2):
+        half = l_ref[which]
+        above = jnp.where(row // fresh < column // fresh, half, 0.0)
+        mirrored = jnp.transpose(above)
+        whole = half + mirrored if which == 0 else half - mirrored
+        moved = jnp.dot(order, whole, precision=lax.Precision.HIGHEST, preferred_element_type=jnp.float32)
+        p_ref[which] = lax.dot_general(
+            moved, order, (((1,), (1,)), ((), ())),
+            precision=lax.Precision.HIGHEST, preferred_element_type=jnp.float32,
+        )[:total]
 
     def slab(k):
         e, a = everyone[k]
@@ -373,7 +383,8 @@
             pltpu.VMEM((2, total, share, 2 * ORDER), jnp.bfloat16),
             pltpu.VMEM((total, 8, 128), jnp.float32),
             pltpu.VMEM((total, 16, depth), jnp.bfloat16),
-            pltpu.VMEM((total, 16, depth), jnp.bfloat16),
+            pltpu.VMEM((2 * ens * GROUP, 16, depth), jnp.bfloat16),
+            pltpu.VMEM((2, 128, 128), jnp.float32),
             pltpu.VMEM((2, total, 128), jnp.float32),
             pltpu.VMEM((ens * amp - 1, 2, circuits, 128), jnp.float32),
             pltpu.SemaphoreType.DMA((groups, 2 * ens - 1)),

time: 80.4 us -> 77 us (0.958)
  Pallas kernels: 71 us -> 67.6 us
    pallas_call x1, Pallas kernels: 71 us -> 67.6 us  [fused(): pl.pallas_call(functools.partial(fused_kernel, layers, ens, amp), out_sha...]
where the time goes in v3:
time: 77 us; the launch traced here: 76.7 us
  Pallas kernels  67.6 us (88%)
  local copies, waits for them, and re-layouts  6.57 us (9%)
  other arithmetic  2.45 us (3%)
    pallas_call x1, Pallas kernels, fused(): pl.pallas_call(functools.partial(fused_kernel, layers, ens, amp), out_sha...  67.6 us
    reshape x1, local copies, waits for them, and re-layouts, fused(): states.reshape(circuits, 2, rows, ORDER)  4.9 us
    sin x1, other arithmetic, small_tables(): return (jnp.cos(angle), jnp.sin(angle), flip)  1.64 us

profile of v3, /device:TPU:0, one launch (start us, length us, event | category | flops | bytes accessed | tf_op | source)
XLA Modules:
  0.0 76.7 jit_solution(18072408446500066365)
XLA Ops:
  0.0 0.0 copy-start
  0.0 0.0 copy-start.1
  0.0 1.6 %fusion = (f32[8,16,7,2]{1,3,2,0:T(2,128)S(1)}, f32[8,16,7,2]{1,3,2,0:T(2,128)S(1)}) fusion(s32[8,16,7,2]{1,3,2,0:T(2,128)} %param.5), kind=kLoop, calls=%fused_computation.1 | loop fusion | flops 3584 | bytes 21504 | tf_op jit(solution)/shard_map/sin | solution.py:163
  1.6 0.4 copy.6
  2.1 0.2 cos.18.cos_ref
  2.3 0.4 copy.7
  2.7 0.2 sin.18.sin_ref
  2.9 0.0 copy-done
  2.9 0.1 copy.8
  3.0 0.1 sub.10.flip_ref
  3.2 0.0 copy-done.1
  3.2 0.1 fusion.6
  3.3 0.1 copy.9
  3.3 0.1 broadcast_in_dim.10.gate_ref
  3.4 4.9 %reshape.51.x_ref = bf16[8,2,512,128]{3,2,1,0:T(8,128)(2,1)S(1)} reshape(bf16[8,2,65536]{2,1,0:T(2,128)(2,1)} %param.4) | data formatting | bytes 4194304 | tf_op jit(solution)/shard_map/reshape | solution.py:400
  8.3 67.6 %shard_map.46 = f32[2,8,128]{2,1,0:T(8,128)S(1)} custom-call(f32[1792]{0:T(1024)S(1)} %cos.18.cos_ref, f32[1792]{0:T(1024)S(1)} %sin.18.sin_ref, f32[768]{0:T(1024)S(1)} %sub.10.flip_ref, f32[8,8,128]{2,1,0:T(8,128)S(1)} %broadcast_in_dim.10.gate_ref, bf16[8,2,512,128]{3,2,1,0:T(8,128)(2,1)S(1)} %reshape.51.x_ref), custom_call_target="tpu_custom_call" | custom-call | tf_op jit(solution)/shard_map/pallas_call | solution.py:375
  76.0 0.1 select_multiply_fusion
  76.1 0.7 dynamic-slice_multiply_fusion
  (3 shorter events, 0.0 us)
Async XLA Ops:
  0.0 2.9 %copy-start = (s32[8,16,6]{1,0,2:T(8,128)S(1)}, s32[8,16,6]{1,0,2:T(8,128)}, u32[]{:S(2)}) copy-start(s32[8,16,6]{1,0,2:T(8,128)} %param.6) | copy-start | bytes 9220
  0.0 3.2 %copy-start.1 = (s32[8,2]{0,1:T(2,128)S(1)}, s32[8,2]{0,1:T(2,128)}, u32[]{:S(2)}) copy-start(s32[8,2]{0,1:T(2,128)} %param.7) | copy-start | bytes 196

commit v4 on v3

--- a/solution.py
+++ b/solution.py
@@ -12,7 +12,7 @@
 TABLE = 64
 ORDER = 2**JOINED
 LOW = 3
-GROUP = 2
+GROUP = 1
 
 
 def from_partner(array, axis, bit):
@@ -108,8 +108,16 @@
     blocks = rows // ORDER
     many = len(t_refs)
     for i in range(many):
-        t_refs[i][:, :ORDER] = x_refs[i][0]
-        t_refs[i][:, ORDER:] = x_refs[i][1]
+
+        def spread(step, carry, i=i):
+            flat = x_refs[i][:, pl.ds(pl.multiple_of(step * 16 * ORDER, 16 * ORDER), 16 * ORDER)]
+            tiles = flat.astype(jnp.float32).reshape(2, 16, ORDER).astype(jnp.bfloat16)
+            rows_at = pl.ds(pl.multiple_of(step * 16, 16), 16)
+            t_refs[i][rows_at, :ORDER] = tiles[0]
+            t_refs[i][rows_at, ORDER:] = tiles[1]
+            return carry
+
+        lax.fori_loop(0, rows // 16, spread, 0, unroll=4)
         build(cos_ref, sin_ref, flip_ref, (first + i) * layers, False, wl_ref.at[i])
 
     def two(pair, carry):
@@ -172,11 +180,11 @@
         functools.partial(layers_kernel, layers),
         grid=(circuits // GROUP,),
         out_shape=jax.ShapeDtypeStruct((circuits, rows, 2 * ORDER), jnp.bfloat16),
-        in_specs=[smem, smem, smem, pl.BlockSpec((GROUP, 2, rows, ORDER), lambda g: (g, 0, 0, 0))],
+        in_specs=[smem, smem, smem, pl.BlockSpec((GROUP, 2, local), lambda g: (g, 0, 0))],
         out_specs=pl.BlockSpec((GROUP, rows, 2 * ORDER), lambda g: (g, 0, 0)),
         scratch_shapes=layers_scratch(rows),
         compiler_params=pltpu.CompilerParams(vmem_limit_bytes=32 << 20),
-    )(*small_tables(layer_angles, entangler), states.reshape(circuits, 2, rows, ORDER))
+    )(*small_tables(layer_angles, entangler), states)
 
 
 MESH_ID = pl.DeviceIdType.MESH
@@ -397,7 +405,7 @@
         compiler_params=pltpu.CompilerParams(
             vmem_limit_bytes=48 << 20, collective_id=0, has_side_effects=True
         ),
-    )(*small_tables(layer_angles, entangler), coefficients, states.reshape(circuits, 2, rows, ORDER))
+    )(*small_tables(layer_angles, entangler), coefficients, states)
 
 
 def finish(summed, states, circuits):

time: 77 us -> 71.4 us (0.927)
  local copies, waits for them, and re-layouts: 6.57 us -> 1.67 us
    reshape x1 -> x0, local copies, waits for them, and re-layouts: 4.9 us -> none  [fused(): states.reshape(circuits, 2, rows, ORDER)]
where the time goes in v4:
time: 71.4 us; the launch traced here: 71.3 us
  Pallas kernels  67 us (94%)
  other arithmetic  2.59 us (4%)
  local copies, waits for them, and re-layouts  1.67 us (2%)
    pallas_call x1, Pallas kernels, fused(): pl.pallas_call(functools.partial(fused_kernel, layers, ens, amp), out_sha...  67 us
    sin x1, other arithmetic, small_tables(): return (jnp.cos(angle), jnp.sin(angle), flip)  1.78 us

profile of v4, /device:TPU:0, one launch (start us, length us, event | category | flops | bytes accessed | tf_op | source)
XLA Modules:
  0.0 71.3 jit_solution(10715906980896816248)
XLA Ops:
  0.0 0.0 copy-start.1
  0.0 0.0 copy-start.2
  0.0 0.0 copy-start
  0.0 1.8 %fusion = (f32[8,16,7,2]{1,3,2,0:T(2,128)S(1)}, f32[8,16,7,2]{1,3,2,0:T(2,128)S(1)}) fusion(s32[8,16,7,2]{1,3,2,0:T(2,128)} %param.5), kind=kLoop, calls=%fused_computation.1 | loop fusion | flops 3584 | bytes 21504 | tf_op jit(solution)/shard_map/sin | solution.py:171
  1.8 0.4 copy.6
  2.2 0.2 cos.18.cos_ref
  2.4 0.4 copy.7
  2.8 0.2 sin.18.sin_ref
  3.0 0.0 copy-done.1
  3.0 0.1 copy.8
  3.2 0.1 sub.10.flip_ref
  3.3 0.0 copy-done.2
  3.3 0.1 fusion.6
  3.4 0.1 copy.9
  3.5 0.1 broadcast_in_dim.10.gate_ref
  3.6 0.0 copy-done
  3.6 67.0 %shard_map.46 = f32[2,8,128]{2,1,0:T(8,128)S(1)} custom-call(f32[1792]{0:T(1024)S(1)} %cos.18.cos_ref, f32[1792]{0:T(1024)S(1)} %sin.18.sin_ref, f32[768]{0:T(1024)S(1)} %sub.10.flip_ref, f32[8,8,128]{2,1,0:T(8,128)S(1)} %broadcast_in_dim.10.gate_ref, bf16[8,2,65536]{2,1,0:T(2,128)(2,1)S(1)} %copy-done), custom_call_target="tpu_custom_call" | custom-call | tf_op jit(solution)/shard_map/pallas_call | solution.py:383
  70.5 0.1 select_multiply_fusion
  70.6 0.7 dynamic-slice_multiply_fusion
  (3 shorter events, 0.0 us)
Async XLA Ops:
  0.0 3.0 %copy-start.1 = (s32[8,16,6]{1,0,2:T(8,128)S(1)}, s32[8,16,6]{1,0,2:T(8,128)}, u32[]{:S(2)}) copy-start(s32[8,16,6]{1,0,2:T(8,128)} %param.6) | copy-start | bytes 9220
  0.0 3.3 %copy-start.2 = (s32[8,2]{0,1:T(2,128)S(1)}, s32[8,2]{0,1:T(2,128)}, u32[]{:S(2)}) copy-start(s32[8,2]{0,1:T(2,128)} %param.7) | copy-start | bytes 196
  0.0 3.6 %copy-start = (bf16[8,2,65536]{2,1,0:T(2,128)(2,1)S(1)}, bf16[8,2,65536]{2,1,0:T(2,128)(2,1)}, u32[]{:S(2)}) copy-start(bf16[8,2,65536]{2,1,0:T(2,128)(2,1)} %x_ref.1) | copy-start | bytes 6291460

commit v5 on v4

--- a/solution.py
+++ b/solution.py
@@ -238,7 +238,7 @@
         gate_copy(k, me).start()
     c_ref[pl.ds(me * circuits, circuits)] = gate_ref[...]
 
-    peers = [(k // ens, k % ens) for k in range(1, 2 * ens)]
+    peers = sorted(((k // ens, k % ens) for k in range(1, 2 * ens)), key=lambda p: (abs(2 * p[1] - ens), p[0]))
 
     def piece(k, group, from_side, from_ens):
         across, along = peers[k]

time: 71.4 us -> 71.1 us (level)
  no operation moved by 1% of the time
where the time goes in v5:
time: 71.1 us; the launch traced here: 71 us
  Pallas kernels  66.7 us (94%)
  other arithmetic  2.59 us (4%)
  local copies, waits for them, and re-layouts  1.67 us (2%)
    pallas_call x1, Pallas kernels, fused(): pl.pallas_call(functools.partial(fused_kernel, layers, ens, amp), out_sha...  66.7 us
    sin x1, other arithmetic, small_tables(): return (jnp.cos(angle), jnp.sin(angle), flip)  1.78 us

profile of v5, /device:TPU:0, one launch (start us, length us, event | category | flops | bytes accessed | tf_op | source)
XLA Modules:
  0.0 71.0 jit_solution(9325666271916515654)
XLA Ops:
  0.0 0.0 copy-start.1
  0.0 0.0 copy-start.2
  0.0 0.0 copy-start
  0.0 1.8 %fusion = (f32[8,16,7,2]{1,3,2,0:T(2,128)S(1)}, f32[8,16,7,2]{1,3,2,0:T(2,128)S(1)}) fusion(s32[8,16,7,2]{1,3,2,0:T(2,128)} %param.5), kind=kLoop, calls=%fused_computation.1 | loop fusion | flops 3584 | bytes 21504 | tf_op jit(solution)/shard_map/sin | solution.py:171
  1.8 0.4 copy.6
  2.2 0.2 cos.18.cos_ref
  2.4 0.4 copy.7
  2.8 0.2 sin.18.sin_ref
  3.0 0.0 copy-done.1
  3.0 0.1 copy.8
  3.2 0.1 sub.10.flip_ref
  3.3 0.0 copy-done.2
  3.3 0.1 fusion.6
  3.4 0.1 copy.9
  3.5 0.1 broadcast_in_dim.10.gate_ref
  3.6 0.0 copy-done
  3.6 66.7 %shard_map.46 = f32[2,8,128]{2,1,0:T(8,128)S(1)} custom-call(f32[1792]{0:T(1024)S(1)} %cos.18.cos_ref, f32[1792]{0:T(1024)S(1)} %sin.18.sin_ref, f32[768]{0:T(1024)S(1)} %sub.10.flip_ref, f32[8,8,128]{2,1,0:T(8,128)S(1)} %broadcast_in_dim.10.gate_ref, bf16[8,2,65536]{2,1,0:T(2,128)(2,1)S(1)} %copy-done), custom_call_target="tpu_custom_call" | custom-call | tf_op jit(solution)/shard_map/pallas_call | solution.py:383
  70.3 0.1 select_multiply_fusion
  70.3 0.7 dynamic-slice_multiply_fusion
  (3 shorter events, 0.0 us)
Async XLA Ops:
  0.0 3.0 %copy-start.1 = (s32[8,16,6]{1,0,2:T(8,128)S(1)}, s32[8,16,6]{1,0,2:T(8,128)}, u32[]{:S(2)}) copy-start(s32[8,16,6]{1,0,2:T(8,128)} %param.6) | copy-start | bytes 9220
  0.0 3.3 %copy-start.2 = (s32[8,2]{0,1:T(2,128)S(1)}, s32[8,2]{0,1:T(2,128)}, u32[]{:S(2)}) copy-start(s32[8,2]{0,1:T(2,128)} %param.7) | copy-start | bytes 196
  0.0 3.6 %copy-start = (bf16[8,2,65536]{2,1,0:T(2,128)(2,1)S(1)}, bf16[8,2,65536]{2,1,0:T(2,128)(2,1)}, u32[]{:S(2)}) copy-start(bf16[8,2,65536]{2,1,0:T(2,128)(2,1)} %x_ref.1) | copy-start | bytes 6291460
